TPU v7x, 512 devices: a whole 4x8x8 slice. The times are simulated.
512 devices in a mesh: seq: 32 (over z_lo, y), tp: 16 (over x, z_hi, core).
Axes of the slice: x: 4, y: 8, z: 8 (z_hi: 2, z_lo: 4; z = z_hi * 4 + z_lo), core: 2. Of those that a mesh axis runs over, the one named last changes fastest.
Arguments:
- latents: bfloat16 [4096, 3072], P('seq', 'tp'), may hold values from -6 to 6
- lengths: int32 [2], replicated, may hold values from 1 to 3072, 4096 in all
- t_index: int32 [2], replicated, may hold values from 0 to 6
- mod_scale: float32 [3072], replicated, may hold values from -2 to 2
- q_weight: bfloat16 [3072, 2048], P(None, 'tp'), may hold values from -0.109375 to 0.109375
- k_weight: bfloat16 [3072, 2048], P(None, 'tp'), may hold values from -0.109375 to 0.109375
- v_weight: bfloat16 [3072, 2048], P(None, 'tp'), may hold values from -0.109375 to 0.109375
- out_weight: bfloat16 [2048, 3072], P('tp'), may hold values from -0.1875 to 0.1875
- q_gain: float32 [128], replicated, may hold values from 0.6 to 2.4
- k_gain: float32 [128], replicated, may hold values from 0.6 to 2.4
- student_weight: bfloat16 [3072, 3072], P('tp'), may hold values from -0.15625 to 0.15625
Outputs:
- target: bfloat16 [4096, 3072], P('seq', 'tp')
- student_velocity: bfloat16 [4096, 3072], P('seq', 'tp')
- loss: float32 [], replicated
Inputs may be any that keep to these rules, and one draw needn't show every extreme that they name: lengths sum to 4096.
All inputs are finite; a program needn't handle non-finite values.
Results may differ from a plain program's by a relative error of at most 0.024.
Values may be sent and summed in bfloat16 or wider, within the bound.
A program may use at most 64 MiB of HBM per device.

v0:
```python
import functools
import math
import jax
import jax.numpy as jnp
from jax import lax
from jax.sharding import Mesh
from jax.sharding import PartitionSpec as P

TGRID = 8
SEQ = ("seq_0", "seq_1")
TP = ("tp_0", "tp_1", "tp_2")
SEQ_TP = ("seq_0", "seq_1", "tp_0", "tp_1", "tp_2")
epsilon = 1e-06
kinetic_weight = 0.1


def in_one_piece(arrays, axis, dim, along):
    widths = [a.shape[along] for a in arrays]
    both = jnp.concatenate(arrays, axis=along)
    whole = lax.all_gather(both, axis, axis=dim, tiled=True)
    return tuple(jnp.split(whole, [sum(widths[:k]) for k in range(1, len(widths))], axis=along))


def from_everyone(value, axis):
    length = lax.axis_size(axis)
    return lax.all_to_all(
        jnp.broadcast_to(value[None], (length, *value.shape)), axis, 0, 0, tiled=True
    )


def laid_out(pieces, dim):
    pieces = jnp.moveaxis(pieces, 0, dim)
    lengths = pieces.shape
    return pieces.reshape(*lengths[:dim], lengths[dim] * lengths[dim + 1], *lengths[dim + 2 :])


def gathered_copies(value, axis, dim):
    pieces = from_everyone(value, axis)
    return laid_out(pieces, dim)


def over_axes(value, axes):
    return functools.reduce(lax.psum, axes, value)


def image_index(positions, image_ends):
    return jnp.sum((positions[:, None] >= image_ends[None, :]).astype(jnp.int32), axis=1)


def head_norm(projected, gain):
    shaped = projected.reshape(projected.shape[0], -1, gain.shape[0])
    normed = shaped * lax.rsqrt(jnp.mean(shaped * shaped, axis=-1, keepdims=True) + epsilon) * gain
    return normed.astype(jnp.bfloat16)


def grouped_columns(whole_left, right_columns, groups):
    row_count = whole_left.shape[0]
    group_width = whole_left.shape[1] // groups
    left_groups = whole_left.reshape(row_count, groups, group_width)
    right_groups = right_columns.reshape(groups, group_width, right_columns.shape[1])
    terms = jnp.einsum(
        "tng,ngd->tnd", left_groups, right_groups, preferred_element_type=jnp.float32
    ).astype(jnp.bfloat16)
    terms = lax.optimization_barrier(terms)
    return jnp.sum(terms.astype(jnp.float32), axis=1)


def teacher(
    state, times, query_image, image_ends, mod_scale, q_weight, k_weight, v_weight, q_gain, k_gain
):
    row_count = state.shape[0]
    head_dim = q_gain.shape[0]
    state32 = state.astype(jnp.float32)
    normed = state32 * lax.rsqrt(jnp.mean(state32 * state32, axis=1, keepdims=True) + epsilon)
    hidden = (normed * (1.0 + times[:, None] * mod_scale[None, :])).astype(jnp.bfloat16)
    queries = head_norm(jnp.dot(hidden, q_weight, preferred_element_type=jnp.float32), q_gain)
    key_rows = head_norm(jnp.dot(hidden, k_weight, preferred_element_type=jnp.float32), k_gain)
    key_rows = key_rows.reshape(row_count, -1)
    value_rows = jnp.dot(hidden, v_weight, preferred_element_type=jnp.float32).astype(jnp.bfloat16)
    heads_here = queries.shape[1]
    score_scale = 1.0 / math.sqrt(head_dim)
    key_block, value_block = in_one_piece((key_rows, value_rows), SEQ, 0, 1)
    running_max = jnp.full((row_count, heads_here), -1e30, jnp.float32)
    count = key_block.shape[0]
    key_image = image_index(jnp.arange(count, dtype=jnp.int32), image_ends)
    key_heads = key_block.reshape(count, heads_here, head_dim)
    value_heads = value_block.reshape(count, heads_here, head_dim)
    same_image = (query_image[:, None] == key_image[None, :])[:, None, :]
    scores = (
        jnp.einsum("qhd,khd->qhk", queries, key_heads, preferred_element_type=jnp.float32)
        * score_scale
    )
    scores = jnp.where(same_image, scores, -1e30)
    new_max = jnp.maximum(running_max, jnp.max(scores, axis=2))
    weights = jnp.where(same_image, jnp.exp(scores - new_max[:, :, None]), 0.0)
    new_total = jnp.sum(weights, axis=2)
    product = jnp.einsum(
        "qhk,khd->qhd",
        weights.astype(jnp.bfloat16),
        value_heads,
        preferred_element_type=jnp.float32,
    )
    mixed = (product / new_total[:, :, None]).astype(jnp.bfloat16).reshape(row_count, -1)
    return (mixed, hidden)


def on_device(
    latents,
    lengths,
    t_index,
    mod_scale,
    q_weight,
    k_weight,
    v_weight,
    out_weight,
    q_gain,
    k_gain,
    student_weight,
):
    row_count, width_here = latents.shape
    tp_count = lax.axis_size(TP)
    image_ends = jnp.cumsum(lengths)
    row_offset = lax.axis_index(SEQ) * row_count
    query_image = image_index(row_offset + jnp.arange(row_count, dtype=jnp.int32), image_ends)
    one_hot = (
        query_image[:, None] == jnp.arange(lengths.shape[0], dtype=jnp.int32)[None, :]
    ).astype(jnp.float32)
    start_times = jnp.sum(one_hot * (t_index.astype(jnp.float32) / TGRID)[None, :], axis=1)
    step_size = 1.0 / TGRID
    whole_rows = lax.all_gather(latents, TP, axis=1, tiled=True)
    velocities = []
    first_hidden = whole_rows
    out_columns, student_columns = (
        lax.all_to_all(out_weight, TP, split_axis=1, concat_axis=0, tiled=True),
        lax.all_to_all(student_weight, TP, split_axis=1, concat_axis=0, tiled=True),
    )
    state_shard = latents
    for euler_index in range(2):
        if euler_index == 1:
            whole_rows = lax.all_gather(state_shard, TP, axis=1, tiled=True)
        mixed, hidden = teacher(
            whole_rows,
            start_times + euler_index * step_size,
            query_image,
            image_ends,
            mod_scale,
            q_weight,
            k_weight,
            v_weight,
            q_gain,
            k_gain,
        )
        if euler_index == 0:
            first_hidden = hidden
        all_heads = gathered_copies(mixed, TP, 1)
        velocity = grouped_columns(all_heads, out_columns, tp_count).astype(jnp.bfloat16)
        velocities.append(velocity)
        state_shard = (
            latents.astype(jnp.float32) + step_size * velocity.astype(jnp.float32)
        ).astype(jnp.bfloat16)
    student_velocity = grouped_columns(first_hidden, student_columns, tp_count).astype(jnp.bfloat16)
    target = (0.5 * (velocities[0].astype(jnp.float32) + velocities[1].astype(jnp.float32))).astype(
        jnp.bfloat16
    )
    student32 = student_velocity.astype(jnp.float32)
    residual = student32 - target.astype(jnp.float32)
    per_token = jnp.sum(residual * residual, axis=1) + kinetic_weight * jnp.sum(
        student32 * student32, axis=1
    )
    image_part = jnp.sum(one_hot * per_token[:, None], axis=0)
    image_sum = over_axes(image_part, SEQ_TP)
    loss = jnp.mean(image_sum / (lengths.astype(jnp.float32) * mod_scale.shape[0]))
    return (target, student_velocity, loss)


def solution(mesh):
    torus = Mesh(mesh.devices.reshape(4, 8, 4, 2, 2), ("seq_0", "seq_1", "tp_0", "tp_1", "tp_2"))
    in_specs = (
        P(SEQ, TP),
        P(),
        P(),
        P(),
        P(None, TP),
        P(None, TP),
        P(None, TP),
        P(TP, None),
        P(),
        P(),
        P(TP, None),
    )
    out_specs = (P(SEQ, TP), P(SEQ, TP), P())
    return jax.shard_map(
        on_device, mesh=torus, in_specs=in_specs, out_specs=out_specs, check_vma=False
    )
```

profile of v0, /device:TPU:1, one launch (start us, length us, event | category | flops | bytes accessed | tf_op | source)
XLA Modules:
  0.0 472.0 jit_solution(12956411148066289239)
XLA Ops:
  7.2 46.2 %all_gather.12 = bf16[128,3072]{0,1:T(8,128)(2,1)S(1)} all-gather(bf16[128,192]{0,1:T(8,128)(2,1)} %param.11), channel_id=1, replica_groups=mesh['seq_0'=4,'seq_1'=8,'tp_0'=4,'tp_1'=2,'tp_2'=2] {'tp_0','tp_1','tp_2'}, dimensions={1}, use_global_device_ids=true | all-gather | bytes 835584 | tf_op jit(solution)/shard_map/all_gather | solution.py:130
  55.6 1.2 fusion.10
  58.4 1.2 copy.19
  59.6 3.6 all-to-all-start.1
  63.2 1.6 multiply_reduce_fusion.2
  64.9 99.5 %all-gather.3.cloned.1.call-done = bf16[4096,256]{0,1:T(8,128)(2,1)} async-done(((bf16[128,256]{0,1:T(8,128)(2,1)}), bf16[4096,256]{0,1:T(8,128)(2,1)}) %all-gather.3.cloned.1.call-update) | async-done | bytes 2097168 | tf_op jit(solution)/shard_map/all_gather | solution.py:20
  164.3 2.3 fusion.72
  166.6 1.9 fusion.4
  168.5 0.9 fusion.29
  169.5 0.9 broadcast_in_dim.20
  170.5 25.1 %all-to-all-start = ((bf16[16,128,128]{2,1,0:T(8,128)(2,1)}), bf16[16,128,128]{2,1,0:T(8,128)(2,1)}, u32[]{:S(2)}, u32[]{:S(2)}) async-start(bf16[16,128,128]{2,1,0:T(8,128)(2,1)} %broadcast_in_dim.20), calls=%async_computation | async-start | bytes 1048576 | tf_op jit(solution)/shard_map/all_to_all | solution.py:26
  195.7 16.0 %all-to-all-done = bf16[16,128,128]{2,1,0:T(8,128)(2,1)} async-done(((bf16[16,128,128]{2,1,0:T(8,128)(2,1)}), bf16[16,128,128]{2,1,0:T(8,128)(2,1)}, u32[]{:S(2)}, u32[]{:S(2)}) %all-to-all-start) | async-done | bytes 524320 | tf_op jit(solution)/shard_map/all_to_all | solution.py:26
  211.7 1.5 fusion.19
  213.3 33.6 %all_gather.14 = bf16[128,3072]{0,1:T(8,128)(2,1)S(1)} all-gather(bf16[128,192]{0,1:T(8,128)(2,1)S(1)} %fusion.51), channel_id=1, replica_groups=mesh['seq_0'=4,'seq_1'=8,'tp_0'=4,'tp_1'=2,'tp_2'=2] {'tp_0','tp_1','tp_2'}, dimensions={1}, use_global_device_ids=true | all-gather | bytes 835584 | tf_op jit(solution)/shard_map/all_gather | solution.py:140
  247.3 2.0 convolution_convert_fusion.2
  250.9 2.5 copy.21
  253.5 9.4 %all-to-all-start.3 = ((bf16[192,16,192]{0,2,1:T(8,128)(2,1)}), bf16[192,16,192]{0,2,1:T(8,128)(2,1)}, u32[]{:S(2)}, u32[]{:S(2)}) async-start(bf16[192,16,192]{0,2,1:T(8,128)(2,1)} %bitcast.82), calls=%async_computation.3 | async-start | bytes 3145728 | tf_op jit(solution)/shard_map/all_to_all | solution.py:135
  262.8 2.0 multiply_reduce_fusion
  264.8 98.7 %all-gather.5.cloned.1.call-done = bf16[4096,256]{0,1:T(8,128)(2,1)} async-done(((bf16[128,256]{0,1:T(8,128)(2,1)}), bf16[4096,256]{0,1:T(8,128)(2,1)}) %all-gather.5.cloned.1.call-update) | async-done | bytes 2097168 | tf_op jit(solution)/shard_map/all_gather | solution.py:20
  363.5 2.3 fusion.73
  365.8 1.9 fusion.6
  367.7 0.9 fusion.28
  368.7 0.9 broadcast_in_dim.22
  369.6 24.2 %all-to-all-start.2 = ((bf16[16,128,128]{2,1,0:T(8,128)(2,1)}), bf16[16,128,128]{2,1,0:T(8,128)(2,1)}, u32[]{:S(2)}, u32[]{:S(2)}) async-start(bf16[16,128,128]{2,1,0:T(8,128)(2,1)} %broadcast_in_dim.22), calls=%async_computation.2 | async-start | bytes 1048576 | tf_op jit(solution)/shard_map/all_to_all | solution.py:26
  393.8 2.0 fusion.21
  395.9 13.0 %all-to-all-done.2 = bf16[16,128,128]{2,1,0:T(8,128)(2,1)} async-done(((bf16[16,128,128]{2,1,0:T(8,128)(2,1)}), bf16[16,128,128]{2,1,0:T(8,128)(2,1)}, u32[]{:S(2)}, u32[]{:S(2)}) %all-to-all-start.2) | async-done | bytes 524320 | tf_op jit(solution)/shard_map/all_to_all | solution.py:26
  408.9 1.5 fusion.20
  411.3 11.7 %psum.35 = f32[2]{0:T(128)S(1)} all-reduce(f32[2]{0:T(128)S(1)} %select_reduce_fusion), channel_id=1, replica_groups=mesh['seq_0'=4,'seq_1'=8,'tp_0'=4,'tp_1'=2,'tp_2'=2] {'seq_0'}, use_global_device_ids=true, to_apply=%region_20.21 | all-reduce | flops 2 | bytes 16 | tf_op jit(solution)/shard_map/psum | solution.py:43
  423.0 13.4 %psum.36 = f32[2]{0:T(128)S(1)} all-reduce(f32[2]{0:T(128)S(1)} %psum.35), channel_id=1, replica_groups=mesh['seq_0'=4,'seq_1'=8,'tp_0'=4,'tp_1'=2,'tp_2'=2] {'seq_1'}, use_global_device_ids=true, to_apply=%region_21.22 | all-reduce | flops 2 | bytes 16 | tf_op jit(solution)/shard_map/psum | solution.py:43
  436.4 6.6 %psum.37 = f32[2]{0:T(128)S(1)} all-reduce(f32[2]{0:T(128)S(1)} %psum.36), channel_id=1, replica_groups=mesh['seq_0'=4,'seq_1'=8,'tp_0'=4,'tp_1'=2,'tp_2'=2] {'tp_0'}, use_global_device_ids=true, to_apply=%region_22.23 | all-reduce | flops 2 | bytes 16 | tf_op jit(solution)/shard_map/psum | solution.py:43
  443.0 7.7 %psum.38 = f32[2]{0:T(128)S(1)} all-reduce(f32[2]{0:T(128)S(1)} %psum.37), channel_id=1, replica_groups=mesh['seq_0'=4,'seq_1'=8,'tp_0'=4,'tp_1'=2,'tp_2'=2] {'tp_1'}, use_global_device_ids=true, to_apply=%region_23.24 | all-reduce | flops 2 | bytes 16 | tf_op jit(solution)/shard_map/psum | solution.py:43
  450.7 12.1 %psum.39 = f32[2]{0:T(128)S(1)} all-reduce(f32[2]{0:T(128)S(1)} %psum.38), channel_id=1, replica_groups=mesh['seq_0'=4,'seq_1'=8,'tp_0'=4,'tp_1'=2,'tp_2'=2] {'tp_2'}, use_global_device_ids=true, to_apply=%region_24.25 | all-reduce | flops 2 | bytes 16 | tf_op jit(solution)/shard_map/psum | solution.py:43
  (62 shorter events, 7.9 us)
Async XLA Ops:
  7.2 50.1 %copy-start = (bf16[3072,128]{1,0:T(8,128)(2,1)S(1)}, bf16[3072,128]{1,0:T(8,128)(2,1)}, u32[]{:S(2)}) copy-start(bf16[3072,128]{1,0:T(8,128)(2,1)} %param.16) | copy-start | bytes 2359300
  7.2 49.6 %copy-start.2 = (bf16[3072,128]{1,0:T(8,128)(2,1)S(1)}, bf16[3072,128]{1,0:T(8,128)(2,1)}, u32[]{:S(2)}) copy-start(bf16[3072,128]{1,0:T(8,128)(2,1)} %param.17) | copy-start | bytes 2359300
  7.2 157.1 %all-gather.3.cloned.1.call-start = ((), (), s32[]{:S(2)}) async-start(), calls=%async_computation.4 | async-start | bytes 2162688 | tf_op jit(solution)/shard_map/all_gather | solution.py:20
  55.6 2.1 copy-start.6
  56.8 1.6 copy-start.1
  58.4 105.9 %copy-start.9 = (f32[128]{0:T(128)S(1)}, f32[128]{0:T(128)}, u32[]{:S(2)}) copy-start(f32[128]{0:T(128)} %param.19) | copy-start | bytes 1540
  59.6 109.9 %all-to-all-start.1 = ((bf16[128,16,192]{0,2,1:T(8,128)(2,1)}), bf16[128,16,192]{0,2,1:T(8,128)(2,1)S(1)}, u32[]{:S(2)}, u32[]{:S(2)}) async-start(bf16[128,16,192]{0,2,1:T(8,128)(2,1)} %bitcast.9), calls=%async_computation.1 | async-start | bytes 1572864 | tf_op jit(solution)/shard_map/all_to_all | solution.py:134
  164.3 4.2 copy-start.8
  170.5 42.8 %copy-start.3 = (bf16[128,192]{0,1:T(8,128)(2,1)S(1)}, bf16[128,192]{0,1:T(8,128)(2,1)}, u32[]{:S(2)}) copy-start(bf16[128,192]{0,1:T(8,128)(2,1)} %param.11) | copy-start | bytes 147460
  170.5 41.2 %all-to-all-start = ((bf16[16,128,128]{2,1,0:T(8,128)(2,1)}), bf16[16,128,128]{2,1,0:T(8,128)(2,1)}, u32[]{:S(2)}, u32[]{:S(2)}) async-start(bf16[16,128,128]{2,1,0:T(8,128)(2,1)} %broadcast_in_dim.20), calls=%async_computation | async-start | bytes 1048576 | tf_op jit(solution)/shard_map/all_to_all | solution.py:26
  195.6 167.9 %all-gather.5.cloned.1.call-start = ((), (), s32[]{:S(2)}) async-start(), calls=%async_computation.5 | async-start | bytes 2162688 | tf_op jit(solution)/shard_map/all_gather | solution.py:20
  195.6 51.7 %copy-start.5 = (f32[3072]{0:T(1024)S(1)}, f32[3072]{0:T(1024)}, u32[]{:S(2)}) copy-start(f32[3072]{0:T(1024)} %param.14) | copy-start | bytes 36868
  253.5 115.2 %all-to-all-start.3 = ((bf16[192,16,192]{0,2,1:T(8,128)(2,1)}), bf16[192,16,192]{0,2,1:T(8,128)(2,1)}, u32[]{:S(2)}, u32[]{:S(2)}) async-start(bf16[192,16,192]{0,2,1:T(8,128)(2,1)} %bitcast.82), calls=%async_computation.3 | async-start | bytes 3145728 | tf_op jit(solution)/shard_map/all_to_all | solution.py:135
  363.5 4.2 copy-start.7
  369.6 39.2 %all-to-all-start.2 = ((bf16[16,128,128]{2,1,0:T(8,128)(2,1)}), bf16[16,128,128]{2,1,0:T(8,128)(2,1)}, u32[]{:S(2)}, u32[]{:S(2)}) async-start(bf16[16,128,128]{2,1,0:T(8,128)(2,1)} %broadcast_in_dim.22), calls=%async_computation.2 | async-start | bytes 1048576 | tf_op jit(solution)/shard_map/all_to_all | solution.py:26
  395.8 67.0 %copy-start.10 = (s32[2]{0:T(128)S(1)}, s32[2]{0:T(128)}, u32[]{:S(2)}) copy-start(s32[2]{0:T(128)} %param.12) | copy-start | bytes 28
  395.9 68.1 %copy-start.4 = (bf16[128,192]{0,1:T(8,128)(2,1)}, bf16[128,192]{0,1:T(8,128)(2,1)S(1)}, u32[]{:S(2)}) copy-start(bf16[128,192]{0,1:T(8,128)(2,1)S(1)} %reduce_sum.188) | copy-start | bytes 147460
Sparse Core Ops, SparseCore 0:
  58.5 105.7 all-gather.2
  251.1 112.4 all-gather.4
where the time goes:
time: 473 us; the launch traced here: 472 us
  waiting for transfers between devices  227 us (48%)
  blocking collectives  131 us (28%)
  starting transfers between devices  62.3 us (13%)
  matrix products  18.5 us (4%)
  between operations  16.1 us (3%)
  other arithmetic  10.8 us (2%)
  local copies, waits for them, and re-layouts  5.83 us (1%)
    all_gather x2, waiting for transfers between devices, in_one_piece(): whole = lax.all_gather(both, axis, axis=dim, tiled=True)  198 us
    psum x5, blocking collectives, over_axes(): return functools.reduce(lax.psum, axes, value)  51.4 us
    all_to_all x2, starting transfers between devices, from_everyone(): lax.all_to_all(jnp.broadcast_to(value[None], (length, *value.shape)), axi...  49.3 us
    all_gather x1, blocking collectives, on_device(): whole_rows = lax.all_gather(latents, TP, axis=1, tiled=True)  46.2 us
    all_gather x1, blocking collectives, on_device(): whole_rows = lax.all_gather(state_shard, TP, axis=1, tiled=True)  33.6 us
    all_to_all x2, waiting for transfers between devices, from_everyone(): lax.all_to_all(jnp.broadcast_to(value[None], (length, *value.shape)), axi...  29 us
  transfers between devices with their start and end apart: 6, of which 4 were waited for; matrix products, arithmetic and copies ran while one was open for 4% of the time, Pallas kernels for 0%

commit v1 on v0

--- a/solution.py
+++ b/solution.py
@@ -127,7 +127,8 @@
     ).astype(jnp.float32)
     start_times = jnp.sum(one_hot * (t_index.astype(jnp.float32) / TGRID)[None, :], axis=1)
     step_size = 1.0 / TGRID
-    whole_rows = lax.all_gather(latents, TP, axis=1, tiled=True)
+    out_arr = lax.all_gather(latents, TP)
+    whole_rows = jnp.concatenate(out_arr, 1)
     velocities = []
     first_hidden = whole_rows
     out_columns, student_columns = (

time: 473 us -> 471 us (level)
  no operation moved by 1% of the time
where the time goes in v1:
time: 471 us; the launch traced here: 470 us
  waiting for transfers between devices  230 us (49%)
  blocking collectives  130 us (28%)
  starting transfers between devices  62.9 us (13%)
  between operations  16.4 us (3%)
  matrix products  15.2 us (3%)
  other arithmetic  9.84 us (2%)
  local copies, waits for them, and re-layouts  6.34 us (1%)
    all_gather x2, waiting for transfers between devices, in_one_piece(): whole = lax.all_gather(both, axis, axis=dim, tiled=True)  202 us
    all_to_all x2, starting transfers between devices, from_everyone(): lax.all_to_all(jnp.broadcast_to(value[None], (length, *value.shape)), axi...  49.8 us
    psum x5, blocking collectives, over_axes(): return functools.reduce(lax.psum, axes, value)  49.6 us
    all_gather x1, blocking collectives, on_device(): out_arr = lax.all_gather(latents, TP)  46.1 us
    all_gather x1, blocking collectives, on_device(): whole_rows = lax.all_gather(state_shard, TP, axis=1, tiled=True)  34.3 us
    all_to_all x2, waiting for transfers between devices, from_everyone(): lax.all_to_all(jnp.broadcast_to(value[None], (length, *value.shape)), axi...  27.9 us
  transfers between devices with their start and end apart: 6, of which 4 were waited for; matrix products, arithmetic and copies ran while one was open for 4% of the time, Pallas kernels for 0%

profile of v1, /device:TPU:1, one launch (start us, length us, event | category | flops | bytes accessed | tf_op | source)
XLA Modules:
  0.0 470.3 jit_solution(896981106944623310)
XLA Ops:
  7.2 0.7 convert_multiply_fusion.4
  8.0 46.1 %all-gather = bf16[2048,192]{0,1:T(8,128)(2,1)S(1)} all-gather(bf16[128,192]{0,1:T(8,128)(2,1)} %param.11), channel_id=2, replica_groups=mesh['seq_0'=4,'seq_1'=8,'tp_0'=4,'tp_1'=2,'tp_2'=2] {'tp_0','tp_1','tp_2'}, dimensions={0}, use_global_device_ids=true | all-gather | bytes 835584 | tf_op jit(solution)/shard_map/all_gather | solution.py:130
  57.1 1.6 convolution_convert_fusion.3
  59.9 1.2 copy.22
  61.1 3.7 all-to-all-start.1
  65.4 100.7 %all-gather.4.cloned.1.call-done = bf16[4096,256]{0,1:T(8,128)(2,1)} async-done(((bf16[128,256]{0,1:T(8,128)(2,1)}), bf16[4096,256]{0,1:T(8,128)(2,1)}) %all-gather.4.cloned.1.call-update) | async-done | bytes 2097168 | tf_op jit(solution)/shard_map/all_gather | solution.py:20
  166.1 2.1 fusion.79
  168.2 1.9 fusion.4
  170.1 0.9 fusion.30
  171.1 0.9 broadcast_in_dim.20
  172.0 24.8 %all-to-all-start = ((bf16[16,128,128]{2,1,0:T(8,128)(2,1)}), bf16[16,128,128]{2,1,0:T(8,128)(2,1)S(1)}, u32[]{:S(2)}, u32[]{:S(2)}) async-start(bf16[16,128,128]{2,1,0:T(8,128)(2,1)} %broadcast_in_dim.20), calls=%async_computation | async-start | bytes 1048576 | tf_op jit(solution)/shard_map/all_to_all | solution.py:26
  196.9 15.4 %all-to-all-done = bf16[16,128,128]{2,1,0:T(8,128)(2,1)S(1)} async-done(((bf16[16,128,128]{2,1,0:T(8,128)(2,1)}), bf16[16,128,128]{2,1,0:T(8,128)(2,1)S(1)}, u32[]{:S(2)}, u32[]{:S(2)}) %all-to-all-start) | async-done | bytes 524320 | tf_op jit(solution)/shard_map/all_to_all | solution.py:26
  212.9 34.3 %all_gather.18 = bf16[128,3072]{0,1:T(8,128)(2,1)S(1)} all-gather(bf16[128,192]{0,1:T(8,128)(2,1)S(1)} %fusion.57), channel_id=1, replica_groups=mesh['seq_0'=4,'seq_1'=8,'tp_0'=4,'tp_1'=2,'tp_2'=2] {'tp_0','tp_1','tp_2'}, dimensions={1}, use_global_device_ids=true | all-gather | bytes 835584 | tf_op jit(solution)/shard_map/all_gather | solution.py:141
  247.7 0.8 convolution_convert_fusion.2
  248.6 1.6 multiply_reduce_fusion.1
  250.9 1.6 copy.25
  252.5 9.3 %all-to-all-start.3 = ((bf16[192,16,192]{0,2,1:T(8,128)(2,1)}), bf16[192,16,192]{0,2,1:T(8,128)(2,1)}, u32[]{:S(2)}, u32[]{:S(2)}) async-start(bf16[192,16,192]{0,2,1:T(8,128)(2,1)} %bitcast.109), calls=%async_computation.3 | async-start | bytes 3145728 | tf_op jit(solution)/shard_map/all_to_all | solution.py:136
  261.9 0.9 multiply_reduce_fusion
  262.7 101.1 %all-gather.6.cloned.1.call-done = bf16[4096,256]{0,1:T(8,128)(2,1)} async-done(((bf16[128,256]{0,1:T(8,128)(2,1)}), bf16[4096,256]{0,1:T(8,128)(2,1)}) %all-gather.6.cloned.1.call-update) | async-done | bytes 2097168 | tf_op jit(solution)/shard_map/all_gather | solution.py:20
  363.8 2.1 fusion.80
  366.0 1.9 fusion.6
  367.8 0.9 fusion.29
  368.9 0.9 broadcast_in_dim.22
  369.8 25.0 %all-to-all-start.2 = ((bf16[16,128,128]{2,1,0:T(8,128)(2,1)}), bf16[16,128,128]{2,1,0:T(8,128)(2,1)S(1)}, u32[]{:S(2)}, u32[]{:S(2)}) async-start(bf16[16,128,128]{2,1,0:T(8,128)(2,1)} %broadcast_in_dim.22), calls=%async_computation.2 | async-start | bytes 1048576 | tf_op jit(solution)/shard_map/all_to_all | solution.py:26
  394.9 2.6 fusion.22
  397.6 12.5 %all-to-all-done.2 = bf16[16,128,128]{2,1,0:T(8,128)(2,1)S(1)} async-done(((bf16[16,128,128]{2,1,0:T(8,128)(2,1)}), bf16[16,128,128]{2,1,0:T(8,128)(2,1)S(1)}, u32[]{:S(2)}, u32[]{:S(2)}) %all-to-all-start.2) | async-done | bytes 524320 | tf_op jit(solution)/shard_map/all_to_all | solution.py:26
  410.7 0.7 fusion.62
  411.5 10.2 %psum.35 = f32[2]{0:T(128)S(1)} all-reduce(f32[2]{0:T(128)S(1)} %select_reduce_fusion), channel_id=1, replica_groups=mesh['seq_0'=4,'seq_1'=8,'tp_0'=4,'tp_1'=2,'tp_2'=2] {'seq_0'}, use_global_device_ids=true, to_apply=%region_20.21 | all-reduce | flops 2 | bytes 16 | tf_op jit(solution)/shard_map/psum | solution.py:43
  421.7 13.2 %psum.36 = f32[2]{0:T(128)S(1)} all-reduce(f32[2]{0:T(128)S(1)} %psum.35), channel_id=1, replica_groups=mesh['seq_0'=4,'seq_1'=8,'tp_0'=4,'tp_1'=2,'tp_2'=2] {'seq_1'}, use_global_device_ids=true, to_apply=%region_21.22 | all-reduce | flops 2 | bytes 16 | tf_op jit(solution)/shard_map/psum | solution.py:43
  434.9 6.6 %psum.37 = f32[2]{0:T(128)S(1)} all-reduce(f32[2]{0:T(128)S(1)} %psum.36), channel_id=1, replica_groups=mesh['seq_0'=4,'seq_1'=8,'tp_0'=4,'tp_1'=2,'tp_2'=2] {'tp_0'}, use_global_device_ids=true, to_apply=%region_22.23 | all-reduce | flops 2 | bytes 16 | tf_op jit(solution)/shard_map/psum | solution.py:43
  441.5 7.7 %psum.38 = f32[2]{0:T(128)S(1)} all-reduce(f32[2]{0:T(128)S(1)} %psum.37), channel_id=1, replica_groups=mesh['seq_0'=4,'seq_1'=8,'tp_0'=4,'tp_1'=2,'tp_2'=2] {'tp_1'}, use_global_device_ids=true, to_apply=%region_23.24 | all-reduce | flops 2 | bytes 16 | tf_op jit(solution)/shard_map/psum | solution.py:43
  449.2 11.9 %psum.39 = f32[2]{0:T(128)S(1)} all-reduce(f32[2]{0:T(128)S(1)} %psum.38), channel_id=1, replica_groups=mesh['seq_0'=4,'seq_1'=8,'tp_0'=4,'tp_1'=2,'tp_2'=2] {'tp_2'}, use_global_device_ids=true, to_apply=%region_24.25 | all-reduce | flops 2 | bytes 16 | tf_op jit(solution)/shard_map/psum | solution.py:43
  (108 shorter events, 8.4 us)
Async XLA Ops:
  7.2 51.6 %copy-start = (bf16[3072,128]{1,0:T(8,128)(2,1)S(1)}, bf16[3072,128]{1,0:T(8,128)(2,1)}, u32[]{:S(2)}) copy-start(bf16[3072,128]{1,0:T(8,128)(2,1)} %param.16) | copy-start | bytes 2359300
  7.2 158.9 %all-gather.4.cloned.1.call-start = ((), (), s32[]{:S(2)}) async-start(), calls=%async_computation.4 | async-start | bytes 2162688 | tf_op jit(solution)/shard_map/all_gather | solution.py:20
  56.5 113.6 %copy-start.16 = (s32[128]{0:T(128)}, s32[128]{0:T(128)S(1)}, u32[]{:S(2)}) copy-start(s32[128]{0:T(128)S(1)} %fusion.68) | copy-start | bytes 1540
  56.6 140.3 %copy-start.20 = (f32[128]{0:T(128)}, f32[128]{0:T(128)S(1)}, u32[]{:S(2)}) copy-start(f32[128]{0:T(128)S(1)} %select_reduce_fusion.1) | copy-start | bytes 1540
  57.1 2.1 copy-start.14
  57.1 2.8 copy-start.3
  59.9 4.9 %copy-start.5 = (bf16[3072,128]{1,0:T(8,128)(2,1)S(1)}, bf16[3072,128]{1,0:T(8,128)(2,1)}, u32[]{:S(2)}) copy-start(bf16[3072,128]{1,0:T(8,128)(2,1)} %param.15) | copy-start | bytes 2359300
  61.1 104.9 %copy-start.24 = (f32[128]{0:T(128)S(1)}, f32[128]{0:T(128)}, u32[]{:S(2)}) copy-start(f32[128]{0:T(128)} %param.19) | copy-start | bytes 1540
  61.1 110.0 %all-to-all-start.1 = ((bf16[128,16,192]{0,2,1:T(8,128)(2,1)}), bf16[128,16,192]{0,2,1:T(8,128)(2,1)S(1)}, u32[]{:S(2)}, u32[]{:S(2)}) async-start(bf16[128,16,192]{0,2,1:T(8,128)(2,1)} %bitcast.11), calls=%async_computation.1 | async-start | bytes 1572864 | tf_op jit(solution)/shard_map/all_to_all | solution.py:135
  168.2 1.9 copy-start.23
  172.0 40.3 %all-to-all-start = ((bf16[16,128,128]{2,1,0:T(8,128)(2,1)}), bf16[16,128,128]{2,1,0:T(8,128)(2,1)S(1)}, u32[]{:S(2)}, u32[]{:S(2)}) async-start(bf16[16,128,128]{2,1,0:T(8,128)(2,1)} %broadcast_in_dim.20), calls=%async_computation | async-start | bytes 1048576 | tf_op jit(solution)/shard_map/all_to_all | solution.py:26
  196.8 16.1 %copy-start.9 = (bf16[128,192]{0,1:T(8,128)(2,1)S(1)}, bf16[128,192]{0,1:T(8,128)(2,1)}, u32[]{:S(2)}) copy-start(bf16[128,192]{0,1:T(8,128)(2,1)} %param.11) | copy-start | bytes 147460
  196.8 167.0 %all-gather.6.cloned.1.call-start = ((), (), s32[]{:S(2)}) async-start(), calls=%async_computation.5 | async-start | bytes 2162688 | tf_op jit(solution)/shard_map/all_gather | solution.py:20
  196.9 50.8 %copy-start.28 = (f32[128]{0:T(128)}, f32[128]{0:T(128)S(1)}, u32[]{:S(2)}) copy-start(f32[128]{0:T(128)S(1)} %broadcast_add_fusion) | copy-start | bytes 1540
  212.7 34.9 %copy-start.4 = (bf16[3072,128]{1,0:T(8,128)(2,1)S(1)}, bf16[3072,128]{1,0:T(8,128)(2,1)}, u32[]{:S(2)}) copy-start(bf16[3072,128]{1,0:T(8,128)(2,1)} %param.17) | copy-start | bytes 2359300
  212.9 34.8 %copy-start.7 = (bf16[128,192]{0,1:T(8,128)(2,1)}, bf16[128,192]{0,1:T(8,128)(2,1)S(1)}, u32[]{:S(2)}) copy-start(bf16[128,192]{0,1:T(8,128)(2,1)S(1)} %reduce_sum.182) | copy-start | bytes 147460
  247.7 2.4 copy-start.30
  248.6 2.3 copy-start.2
  252.5 9.3 %copy-start.6 = (bf16[3072,128]{1,0:T(8,128)(2,1)S(1)}, bf16[3072,128]{1,0:T(8,128)(2,1)}, u32[]{:S(2)}) copy-start(bf16[3072,128]{1,0:T(8,128)(2,1)} %param.15) | copy-start | bytes 2359300
  252.5 9.3 %copy-start.13 = (f32[3072]{0:T(1024)S(1)}, f32[3072]{0:T(1024)}, u32[]{:S(2)}) copy-start(f32[3072]{0:T(1024)} %param.14) | copy-start | bytes 36868
  252.5 9.3 %copy-start.29 = (f32[128]{0:T(128)S(1)}, f32[128]{0:T(128)}, u32[]{:S(2)}) copy-start(f32[128]{0:T(128)} %copy-done.28) | copy-start | bytes 1540
  252.5 9.3 %copy-start.31 = (f32[128]{0:T(128)S(1)}, f32[128]{0:T(128)}, u32[]{:S(2)}) copy-start(f32[128]{0:T(128)} %copy-done.30) | copy-start | bytes 1540
  252.5 116.3 %all-to-all-start.3 = ((bf16[192,16,192]{0,2,1:T(8,128)(2,1)}), bf16[192,16,192]{0,2,1:T(8,128)(2,1)}, u32[]{:S(2)}, u32[]{:S(2)}) async-start(bf16[192,16,192]{0,2,1:T(8,128)(2,1)} %bitcast.109), calls=%async_computation.3 | async-start | bytes 3145728 | tf_op jit(solution)/shard_map/all_to_all | solution.py:136
  261.8 102.0 %copy-start.17 = (s32[128]{0:T(128)S(1)}, s32[128]{0:T(128)}, u32[]{:S(2)}) copy-start(s32[128]{0:T(128)} %copy-done.16) | copy-start | bytes 1540
  261.8 101.9 %copy-start.25 = (f32[128]{0:T(128)S(1)}, f32[128]{0:T(128)}, u32[]{:S(2)}) copy-start(f32[128]{0:T(128)} %param.19) | copy-start | bytes 1540
  365.9 1.9 copy-start.22
  368.7 26.2 %copy-start.19 = (f32[128]{0:T(128)S(1)}, f32[128]{0:T(128)}, u32[]{:S(2)}) copy-start(f32[128]{0:T(128)} %copy-done.18) | copy-start | bytes 1540
  368.7 26.2 %copy-start.21 = (f32[128]{0:T(128)S(1)}, f32[128]{0:T(128)}, u32[]{:S(2)}) copy-start(f32[128]{0:T(128)} %copy-done.20) | copy-start | bytes 1540
  369.8 40.3 %all-to-all-start.2 = ((bf16[16,128,128]{2,1,0:T(8,128)(2,1)}), bf16[16,128,128]{2,1,0:T(8,128)(2,1)S(1)}, u32[]{:S(2)}, u32[]{:S(2)}) async-start(bf16[16,128,128]{2,1,0:T(8,128)(2,1)} %broadcast_in_dim.22), calls=%async_computation.2 | async-start | bytes 1048576 | tf_op jit(solution)/shard_map/all_to_all | solution.py:26
  397.6 51.6 %copy-start.10 = (bf16[128,192]{0,1:T(8,128)(2,1)}, bf16[128,192]{0,1:T(8,128)(2,1)S(1)}, u32[]{:S(2)}) copy-start(bf16[128,192]{0,1:T(8,128)(2,1)S(1)} %reduce_sum.188) | copy-start | bytes 147460
  397.6 13.1 %copy-start.8 = (bf16[128,192]{0,1:T(8,128)(2,1)S(1)}, bf16[128,192]{0,1:T(8,128)(2,1)}, u32[]{:S(2)}) copy-start(bf16[128,192]{0,1:T(8,128)(2,1)} %copy-done.7) | copy-start | bytes 147460
  397.6 63.5 %copy-start.27 = (s32[2]{0:T(128)S(1)}, s32[2]{0:T(128)}, u32[]{:S(2)}) copy-start(s32[2]{0:T(128)} %param.12) | copy-start | bytes 28
  (6 other events, 6.8 us)
Sparse Core Ops, SparseCore 0:
  60.0 105.9 all-gather.3
  251.0 112.7 all-gather.5
